TPU v7x, 256 devices: a whole 4x4x8 slice. The times are simulated.
256 devices in a mesh: depth: 8 (over x, y_lo), lat: 32 (over y_hi, z, core).
Axes of the slice: x: 4, y: 4 (y_hi: 2, y_lo: 2; y = y_hi * 2 + y_lo), z: 8, core: 2. Of those that a mesh axis runs over, the one named last changes fastest.
Arguments:
- source: float32 [8, 32, 768, 64], P('depth', 'lat'), may hold values from -6 to 6
- rate: float32 [8, 32, 768], P('depth', 'lat'), may hold values from 0.002 to 2
- lat_op: float32 [8, 32, 768, 768], P('depth', 'lat'), may hold values from -1 to 1.5
- down_op: float32 [8, 32, 768, 768], P('depth', 'lat'), may hold values from -1 to 1.5
- up_op: float32 [8, 32, 768, 768], P('depth', 'lat'), may hold values from -1 to 1.5
Outputs:
- traces: float32 [8, 32, 768, 64], P('depth', 'lat')
All inputs are finite; a program needn't handle non-finite values.
Results may differ from a plain program's by a relative error of at most 0.0001.
Values sent between devices are 32-bit elements; how exact they have to be, the bound alone decides.
A program may use at most 128 MiB of HBM per device.

v0:
```python
import jax
import jax.numpy as jnp
from jax import lax
from jax.sharding import PartitionSpec as P

PASSES = 2


lateral_weight = 0.1
depth_weight = 0.25
relax_weight = 0.5


def passed_along(value, axis, steps):
    count = lax.axis_size(axis)
    leading, last = (max(0, -steps), min(count, count - steps))
    return lax.ppermute(value, axis, [(source, source + steps) for source in range(leading, last)])


def carried_in(part, axis, combine, identity, reverse):
    count = lax.axis_size(axis)
    place = lax.axis_index(axis)
    ahead = count - 1 - place if reverse else place
    gathered = jax.tree.map(lambda a: lax.all_gather(a, axis), part)
    state = jax.tree.map(lambda a, e: jnp.zeros_like(a) + jnp.asarray(e, a.dtype), part, identity)

    def one(hop, state):
        source = count - 1 - hop if reverse else hop
        return combine(
            state, jax.tree.map(lambda a: lax.dynamic_index_in_dim(a, source, 0, False), gathered)
        )

    return lax.fori_loop(0, ahead, one, state)


def propagate(matrix, vectors):
    return jnp.dot(
        matrix, vectors, precision=lax.Precision.HIGHEST, preferred_element_type=jnp.float32
    )


def linked(earlier, later_part):
    return (earlier[0] * later_part[0], later_part[0][:, None] * earlier[1] + later_part[1])


def chain_down(matrix, smoothed):

    def advance(position, carried):
        return passed_along(propagate(matrix, carried) + smoothed, "depth", 1)

    return lax.fori_loop(0, lax.axis_size("depth") - 1, advance, jnp.zeros_like(smoothed))


def chain_up(matrix, smoothed):

    def advance(position, carried):
        return passed_along(propagate(matrix, carried) + smoothed, "depth", -1)

    return lax.fori_loop(0, lax.axis_size("depth") - 1, advance, jnp.zeros_like(smoothed))


def shards(source, rate, lat_op, down_op, up_op):
    order = source.shape[2]
    columns = source.shape[3]
    source_trace = source.reshape(order, columns)
    decay = jnp.exp(-rate.reshape(order))
    lateral = lat_op.reshape(order, order)
    lower_matrix = down_op.reshape(order, order)
    upper_matrix = up_op.reshape(order, order)
    identity_pair = (jnp.ones_like(decay), jnp.zeros_like(source_trace))
    traces = jnp.zeros_like(source_trace)
    anchor = source_trace + relax_weight * traces
    smoothed = anchor
    for pass_turn in range(PASSES):
        lifted = propagate(lateral, smoothed)
        rightward = carried_in((decay, lifted), "lat", linked, identity_pair, False)
        leftward = carried_in((decay, lifted), "lat", linked, identity_pair, True)
        right_full = decay[:, None] * rightward[1] + lifted
        left_full = decay[:, None] * leftward[1] + lifted
        smoothed = anchor + lateral_weight * (right_full + left_full)
    downward = chain_down(lower_matrix, smoothed)
    upward = chain_up(upper_matrix, smoothed)
    traces = smoothed + depth_weight * (downward + upward)
    return traces.reshape(1, 1, order, columns)


def solution(mesh):
    in_specs = (
        P("depth", "lat", None, None),
        P("depth", "lat", None),
        P("depth", "lat", None, None),
        P("depth", "lat", None, None),
        P("depth", "lat", None, None),
    )
    out_specs = P("depth", "lat", None, None)
    return jax.shard_map(shards, mesh=mesh, in_specs=in_specs, out_specs=out_specs, check_vma=False)
```

profile of v0, /device:TPU:16, one launch (start us, length us, event | category | flops | bytes accessed | tf_op | source)
XLA Modules:
  0.0 506.0 jit_solution(7032718764020626057)
XLA Ops:
  12.3 42.3 %all-gather = f32[32,1,768]{2,1,0:T(1,128)S(1)} all-gather(f32[1,1,768]{2,1,0:T(1,128)S(1)} %get-tuple-element.408), channel_id=2, replica_groups=mesh['depth'=8,'lat'=32] {'lat'}, dimensions={0}, use_global_device_ids=true | all-gather | bytes 101376 | tf_op jit(solution)/shard_map/all_gather | solution.py:24
  54.5 51.8 %all-gather.6.cloned.1.call-done = f32[24576,64]{0,1:T(8,128)} async-done(((f32[768,64]{0,1:T(8,128)}), f32[24576,64]{0,1:T(8,128)}) %all-gather.6.cloned.1.call-update) | async-done | bytes 6291472 | tf_op jit(solution)/shard_map/all_gather | solution.py:24
  106.3 9.6 %copy.31 = f32[24576,64]{1,0:T(8,128)} copy(f32[24576,64]{0,1:T(8,128)} %all-gather.6.cloned.1.call-done) | data formatting | bytes 12582912 | tf_op jit(solution)/shard_map/while | solution.py:33
  115.9 18.6 %while.73 = (s32[]{:T(128)}, f32[768,64]{1,0:T(8,128)S(1)}, s32[]{:T(128)}, f32[32,768]{1,0:T(8,128)S(1)}, f32[32,768,64]{2,1,0:T(8,128)}, /*index=5*/s32[]{:T(128)}, s32[]{:T(128)}, s32[]{:T(128)}, s32[]{:T(128)}) while((s32[]{:T(128)}, f32[768,64]{1,0:T(8,128)S(1)}, s32[]{:T(128)}, f32[32,768]{1,0:T(8,128)S(1)}, f32[32,768,64]{2,1,0:T(8,128)}, ...), condition=%wide.region_3.4_spmd, body=%wide.region_2.3_spmd.sunk | while | flops 98310 | bytes 599187 | solution.py:33
  134.7 20.0 %while.72 = (s32[]{:T(128)}, f32[768,64]{1,0:T(8,128)S(1)}, s32[]{:T(128)}, f32[32,768]{1,0:T(8,128)S(1)}, f32[32,768,64]{2,1,0:T(8,128)}, /*index=5*/s32[]{:T(128)}, s32[]{:T(128)}, s32[]{:T(128)}) while((s32[]{:T(128)}, f32[768,64]{1,0:T(8,128)S(1)}, s32[]{:T(128)}, f32[32,768]{1,0:T(8,128)S(1)}, f32[32,768,64]{2,1,0:T(8,128)}, ...), condition=%wide.region_1.2_spmd, body=%wide.region_0.1_spmd.sunk | while | flops 98309 | bytes 599167 | solution.py:33
  158.5 90.5 %all-gather.8.cloned.1.call-done = f32[24576,64]{0,1:T(8,128)} async-done(((f32[768,64]{0,1:T(8,128)}), f32[24576,64]{0,1:T(8,128)}) %all-gather.8.cloned.1.call-update) | async-done | bytes 6291472 | tf_op jit(solution)/shard_map/all_gather | solution.py:24
  248.9 9.6 %copy.32 = f32[24576,64]{1,0:T(8,128)} copy(f32[24576,64]{0,1:T(8,128)} %all-gather.8.cloned.1.call-done) | data formatting | bytes 12582912 | tf_op jit(solution)/shard_map/while | solution.py:33
  258.5 29.6 %while.75 = (s32[]{:T(128)}, f32[768,64]{1,0:T(8,128)S(1)}, s32[]{:T(128)}, f32[32,768]{1,0:T(8,128)}, f32[32,768,64]{2,1,0:T(8,128)}, /*index=5*/s32[]{:T(128)}, s32[]{:T(128)}, s32[]{:T(128)}, s32[]{:T(128)}) while((s32[]{:T(128)}, f32[768,64]{1,0:T(8,128)S(1)}, s32[]{:T(128)}, f32[32,768]{1,0:T(8,128)}, f32[32,768,64]{2,1,0:T(8,128)}, ...), condition=%wide.region_7.8_spmd, body=%wide.region_6.7_spmd.sunk | while | flops 98310 | bytes 599187 | solution.py:33
  288.3 31.7 %while.74 = (s32[]{:T(128)}, f32[768,64]{1,0:T(8,128)S(1)}, s32[]{:T(128)}, f32[32,768]{1,0:T(8,128)}, f32[32,768,64]{2,1,0:T(8,128)}, /*index=5*/s32[]{:T(128)}, s32[]{:T(128)}, s32[]{:T(128)}) while((s32[]{:T(128)}, f32[768,64]{1,0:T(8,128)S(1)}, s32[]{:T(128)}, f32[32,768]{1,0:T(8,128)}, f32[32,768,64]{2,1,0:T(8,128)}, ...), condition=%wide.region_5.6_spmd, body=%wide.region_4.5_spmd.sunk | while | flops 98309 | bytes 599167 | solution.py:33
  320.3 85.3 %while.76 = (s32[]{:T(128)}, f32[768,64]{0,1:T(8,128)S(1)}, f32[768,768]{1,0:T(8,128)}, f32[768,64]{0,1:T(8,128)S(1)}, s32[]{:T(128)}) while((s32[]{:T(128)}, f32[768,64]{0,1:T(8,128)S(1)}, f32[768,768]{1,0:T(8,128)}, f32[768,64]{0,1:T(8,128)S(1)}, s32[]{:T(128)}) %tuple.142), condition=%wide.region_9.10_spmd, body=%wide.region_8.9_spmd.sunk | while | flops 453033984 | bytes 3735653 | solution.py:51
  328.3 4.5 collective-permute-done
  336.8 4.4 collective-permute-start
  360.5 4.5 collective-permute-start
  372.2 5.3 %collective-permute-start = (f32[768,64]{0,1:T(8,128)S(1)}, f32[768,64]{0,1:T(8,128)S(1)}, u32[]{:S(2)}, u32[]{:S(2)}) collective-permute-start(f32[768,64]{0,1:T(8,128)S(1)} %convolution_add_fusion.4), channel_id=1, source_target_pairs={{0,32},{32,64},{64,96},{96,128},{128,160},{160,192},{192,224},{1,3... | collective-permute-start | bytes 589832 | tf_op jit(solution)/shard_map/while/body/eval_jaxpr/ppermute | solution.py:17
  384.7 5.3 %collective-permute-start = (f32[768,64]{0,1:T(8,128)S(1)}, f32[768,64]{0,1:T(8,128)S(1)}, u32[]{:S(2)}, u32[]{:S(2)}) collective-permute-start(f32[768,64]{0,1:T(8,128)S(1)} %convolution_add_fusion.4), channel_id=1, source_target_pairs={{0,32},{32,64},{64,96},{96,128},{128,160},{160,192},{192,224},{1,3... | collective-permute-start | bytes 589832 | tf_op jit(solution)/shard_map/while/body/eval_jaxpr/ppermute | solution.py:17
  397.1 5.3 %collective-permute-start = (f32[768,64]{0,1:T(8,128)S(1)}, f32[768,64]{0,1:T(8,128)S(1)}, u32[]{:S(2)}, u32[]{:S(2)}) collective-permute-start(f32[768,64]{0,1:T(8,128)S(1)} %convolution_add_fusion.4), channel_id=1, source_target_pairs={{0,32},{32,64},{64,96},{96,128},{128,160},{160,192},{192,224},{1,3... | collective-permute-start | bytes 589832 | tf_op jit(solution)/shard_map/while/body/eval_jaxpr/ppermute | solution.py:17
  405.6 92.8 %while.77 = (s32[]{:T(128)}, f32[768,64]{0,1:T(8,128)S(1)}, f32[768,768]{1,0:T(8,128)}, f32[768,64]{0,1:T(8,128)S(1)}, s32[]{:T(128)}) while((s32[]{:T(128)}, f32[768,64]{0,1:T(8,128)S(1)}, f32[768,768]{1,0:T(8,128)}, f32[768,64]{0,1:T(8,128)S(1)}, s32[]{:T(128)}) %tuple.144), condition=%wide.region_11.12_spmd, body=%wide.region_10.11_spmd.sunk | while | flops 453033984 | bytes 3735653 | solution.py:59
  410.9 7.6 %collective-permute-done.1 = f32[768,64]{0,1:T(8,128)S(1)} collective-permute-done((f32[768,64]{0,1:T(8,128)S(1)}, f32[768,64]{0,1:T(8,128)S(1)}, u32[]{:S(2)}, u32[]{:S(2)}) %collective-permute-start.1) | collective-permute-done | bytes 196640 | tf_op jit(solution)/shard_map/while/body/eval_jaxpr/ppermute | solution.py:17
  423.9 7.6 %collective-permute-done.1 = f32[768,64]{0,1:T(8,128)S(1)} collective-permute-done((f32[768,64]{0,1:T(8,128)S(1)}, f32[768,64]{0,1:T(8,128)S(1)}, u32[]{:S(2)}, u32[]{:S(2)}) %collective-permute-start.1) | collective-permute-done | bytes 196640 | tf_op jit(solution)/shard_map/while/body/eval_jaxpr/ppermute | solution.py:17
  436.8 7.9 %collective-permute-done.1 = f32[768,64]{0,1:T(8,128)S(1)} collective-permute-done((f32[768,64]{0,1:T(8,128)S(1)}, f32[768,64]{0,1:T(8,128)S(1)}, u32[]{:S(2)}, u32[]{:S(2)}) %collective-permute-start.1) | collective-permute-done | bytes 196640 | tf_op jit(solution)/shard_map/while/body/eval_jaxpr/ppermute | solution.py:17
  450.0 9.3 %collective-permute-done.1 = f32[768,64]{0,1:T(8,128)S(1)} collective-permute-done((f32[768,64]{0,1:T(8,128)S(1)}, f32[768,64]{0,1:T(8,128)S(1)}, u32[]{:S(2)}, u32[]{:S(2)}) %collective-permute-start.1) | collective-permute-done | bytes 196640 | tf_op jit(solution)/shard_map/while/body/eval_jaxpr/ppermute | solution.py:17
  464.6 8.8 %collective-permute-done.1 = f32[768,64]{0,1:T(8,128)S(1)} collective-permute-done((f32[768,64]{0,1:T(8,128)S(1)}, f32[768,64]{0,1:T(8,128)S(1)}, u32[]{:S(2)}, u32[]{:S(2)}) %collective-permute-start.1) | collective-permute-done | bytes 196640 | tf_op jit(solution)/shard_map/while/body/eval_jaxpr/ppermute | solution.py:17
  478.7 7.5 %collective-permute-done.1 = f32[768,64]{0,1:T(8,128)S(1)} collective-permute-done((f32[768,64]{0,1:T(8,128)S(1)}, f32[768,64]{0,1:T(8,128)S(1)}, u32[]{:S(2)}, u32[]{:S(2)}) %collective-permute-start.1) | collective-permute-done | bytes 196640 | tf_op jit(solution)/shard_map/while/body/eval_jaxpr/ppermute | solution.py:17
  491.6 6.9 %collective-permute-done.1 = f32[768,64]{0,1:T(8,128)S(1)} collective-permute-done((f32[768,64]{0,1:T(8,128)S(1)}, f32[768,64]{0,1:T(8,128)S(1)}, u32[]{:S(2)}, u32[]{:S(2)}) %collective-permute-start.1) | collective-permute-done | bytes 196640 | tf_op jit(solution)/shard_map/while/body/eval_jaxpr/ppermute | solution.py:17
  (185 shorter events, 201.3 us)
Async XLA Ops:
  6.5 1.7 copy-start
  6.5 5.7 %copy-start.5 = (f32[1,1,768]{2,1,0:T(1,128)S(1)}, f32[1,1,768]{2,1,0:T(1,128)}, u32[]{:S(2)}) copy-start(f32[1,1,768]{2,1,0:T(1,128)} %param.18) | copy-start | bytes 9220
  6.5 99.7 %all-gather.6.cloned.1.call-start = ((), (), s32[]{:S(2)}) async-start(), calls=%async_computation | async-start | bytes 6488064 | tf_op jit(solution)/shard_map/all_gather | solution.py:24
  12.2 236.8 %all-gather.8.cloned.1.call-start = ((), (), s32[]{:S(2)}) async-start(), calls=%async_computation.1 | async-start | bytes 6488064 | tf_op jit(solution)/shard_map/all_gather | solution.py:24
  134.7 20.8 %copy-start.2 = (f32[768,64]{0,1:T(8,128)S(1)}, f32[768,64]{0,1:T(8,128)}, u32[]{:S(2)}) copy-start(f32[768,64]{0,1:T(8,128)} %fusion.2) | copy-start | bytes 589828
  134.7 20.8 %copy-start.3 = (f32[1,1,768,64]{2,3,1,0:T(8,128)S(1)}, f32[1,1,768,64]{2,3,1,0:T(8,128)}, u32[]{:S(2)}) copy-start(f32[1,1,768,64]{2,3,1,0:T(8,128)} %param.17) | copy-start | bytes 589828
  154.7 0.6 copy-start.4
  288.3 31.8 %copy-start.1 = (f32[768,64]{0,1:T(8,128)S(1)}, f32[768,64]{0,1:T(8,128)}, u32[]{:S(2)}) copy-start(f32[768,64]{0,1:T(8,128)} %fusion.4) | copy-start | bytes 589828
  324.3 8.6 %collective-permute-start = (f32[768,64]{0,1:T(8,128)S(1)}, f32[768,64]{0,1:T(8,128)S(1)}, u32[]{:S(2)}, u32[]{:S(2)}) collective-permute-start(f32[768,64]{0,1:T(8,128)S(1)} %convolution_add_fusion.4), channel_id=1, source_target_pairs={{0,32},{32,64},{64,96},{96,128},{128,160},{160,192},{192,224},{1,3... | collective-permute-start | bytes 589832 | tf_op jit(solution)/shard_map/while/body/eval_jaxpr/ppermute | solution.py:17
  336.8 8.1 %collective-permute-start = (f32[768,64]{0,1:T(8,128)S(1)}, f32[768,64]{0,1:T(8,128)S(1)}, u32[]{:S(2)}, u32[]{:S(2)}) collective-permute-start(f32[768,64]{0,1:T(8,128)S(1)} %convolution_add_fusion.4), channel_id=1, source_target_pairs={{0,32},{32,64},{64,96},{96,128},{128,160},{160,192},{192,224},{1,3... | collective-permute-start | bytes 589832 | tf_op jit(solution)/shard_map/while/body/eval_jaxpr/ppermute | solution.py:17
  348.9 7.6 %collective-permute-start = (f32[768,64]{0,1:T(8,128)S(1)}, f32[768,64]{0,1:T(8,128)S(1)}, u32[]{:S(2)}, u32[]{:S(2)}) collective-permute-start(f32[768,64]{0,1:T(8,128)S(1)} %convolution_add_fusion.4), channel_id=1, source_target_pairs={{0,32},{32,64},{64,96},{96,128},{128,160},{160,192},{192,224},{1,3... | collective-permute-start | bytes 589832 | tf_op jit(solution)/shard_map/while/body/eval_jaxpr/ppermute | solution.py:17
  360.5 7.7 %collective-permute-start = (f32[768,64]{0,1:T(8,128)S(1)}, f32[768,64]{0,1:T(8,128)S(1)}, u32[]{:S(2)}, u32[]{:S(2)}) collective-permute-start(f32[768,64]{0,1:T(8,128)S(1)} %convolution_add_fusion.4), channel_id=1, source_target_pairs={{0,32},{32,64},{64,96},{96,128},{128,160},{160,192},{192,224},{1,3... | collective-permute-start | bytes 589832 | tf_op jit(solution)/shard_map/while/body/eval_jaxpr/ppermute | solution.py:17
  372.2 8.5 %collective-permute-start = (f32[768,64]{0,1:T(8,128)S(1)}, f32[768,64]{0,1:T(8,128)S(1)}, u32[]{:S(2)}, u32[]{:S(2)}) collective-permute-start(f32[768,64]{0,1:T(8,128)S(1)} %convolution_add_fusion.4), channel_id=1, source_target_pairs={{0,32},{32,64},{64,96},{96,128},{128,160},{160,192},{192,224},{1,3... | collective-permute-start | bytes 589832 | tf_op jit(solution)/shard_map/while/body/eval_jaxpr/ppermute | solution.py:17
  384.7 8.5 %collective-permute-start = (f32[768,64]{0,1:T(8,128)S(1)}, f32[768,64]{0,1:T(8,128)S(1)}, u32[]{:S(2)}, u32[]{:S(2)}) collective-permute-start(f32[768,64]{0,1:T(8,128)S(1)} %convolution_add_fusion.4), channel_id=1, source_target_pairs={{0,32},{32,64},{64,96},{96,128},{128,160},{160,192},{192,224},{1,3... | collective-permute-start | bytes 589832 | tf_op jit(solution)/shard_map/while/body/eval_jaxpr/ppermute | solution.py:17
  397.1 8.5 %collective-permute-start = (f32[768,64]{0,1:T(8,128)S(1)}, f32[768,64]{0,1:T(8,128)S(1)}, u32[]{:S(2)}, u32[]{:S(2)}) collective-permute-start(f32[768,64]{0,1:T(8,128)S(1)} %convolution_add_fusion.4), channel_id=1, source_target_pairs={{0,32},{32,64},{64,96},{96,128},{128,160},{160,192},{192,224},{1,3... | collective-permute-start | bytes 589832 | tf_op jit(solution)/shard_map/while/body/eval_jaxpr/ppermute | solution.py:17
  409.6 8.9 %collective-permute-start.1 = (f32[768,64]{0,1:T(8,128)S(1)}, f32[768,64]{0,1:T(8,128)S(1)}, u32[]{:S(2)}, u32[]{:S(2)}) collective-permute-start(f32[768,64]{0,1:T(8,128)S(1)} %convolution_add_fusion.5), channel_id=1, source_target_pairs={{32,0},{64,32},{96,64},{128,96},{160,128},{192,160},{224,192},{33,... | collective-permute-start | bytes 589832 | tf_op jit(solution)/shard_map/while/body/eval_jaxpr/ppermute | solution.py:17
  422.6 8.9 %collective-permute-start.1 = (f32[768,64]{0,1:T(8,128)S(1)}, f32[768,64]{0,1:T(8,128)S(1)}, u32[]{:S(2)}, u32[]{:S(2)}) collective-permute-start(f32[768,64]{0,1:T(8,128)S(1)} %convolution_add_fusion.5), channel_id=1, source_target_pairs={{32,0},{64,32},{96,64},{128,96},{160,128},{192,160},{224,192},{33,... | collective-permute-start | bytes 589832 | tf_op jit(solution)/shard_map/while/body/eval_jaxpr/ppermute | solution.py:17
  435.5 9.2 %collective-permute-start.1 = (f32[768,64]{0,1:T(8,128)S(1)}, f32[768,64]{0,1:T(8,128)S(1)}, u32[]{:S(2)}, u32[]{:S(2)}) collective-permute-start(f32[768,64]{0,1:T(8,128)S(1)} %convolution_add_fusion.5), channel_id=1, source_target_pairs={{32,0},{64,32},{96,64},{128,96},{160,128},{192,160},{224,192},{33,... | collective-permute-start | bytes 589832 | tf_op jit(solution)/shard_map/while/body/eval_jaxpr/ppermute | solution.py:17
  448.7 10.6 %collective-permute-start.1 = (f32[768,64]{0,1:T(8,128)S(1)}, f32[768,64]{0,1:T(8,128)S(1)}, u32[]{:S(2)}, u32[]{:S(2)}) collective-permute-start(f32[768,64]{0,1:T(8,128)S(1)} %convolution_add_fusion.5), channel_id=1, source_target_pairs={{32,0},{64,32},{96,64},{128,96},{160,128},{192,160},{224,192},{33,... | collective-permute-start | bytes 589832 | tf_op jit(solution)/shard_map/while/body/eval_jaxpr/ppermute | solution.py:17
  463.3 10.1 %collective-permute-start.1 = (f32[768,64]{0,1:T(8,128)S(1)}, f32[768,64]{0,1:T(8,128)S(1)}, u32[]{:S(2)}, u32[]{:S(2)}) collective-permute-start(f32[768,64]{0,1:T(8,128)S(1)} %convolution_add_fusion.5), channel_id=1, source_target_pairs={{32,0},{64,32},{96,64},{128,96},{160,128},{192,160},{224,192},{33,... | collective-permute-start | bytes 589832 | tf_op jit(solution)/shard_map/while/body/eval_jaxpr/ppermute | solution.py:17
  477.4 8.8 %collective-permute-start.1 = (f32[768,64]{0,1:T(8,128)S(1)}, f32[768,64]{0,1:T(8,128)S(1)}, u32[]{:S(2)}, u32[]{:S(2)}) collective-permute-start(f32[768,64]{0,1:T(8,128)S(1)} %convolution_add_fusion.5), channel_id=1, source_target_pairs={{32,0},{64,32},{96,64},{128,96},{160,128},{192,160},{224,192},{33,... | collective-permute-start | bytes 589832 | tf_op jit(solution)/shard_map/while/body/eval_jaxpr/ppermute | solution.py:17
  490.3 8.2 %collective-permute-start.1 = (f32[768,64]{0,1:T(8,128)S(1)}, f32[768,64]{0,1:T(8,128)S(1)}, u32[]{:S(2)}, u32[]{:S(2)}) collective-permute-start(f32[768,64]{0,1:T(8,128)S(1)} %convolution_add_fusion.5), channel_id=1, source_target_pairs={{32,0},{64,32},{96,64},{128,96},{160,128},{192,160},{224,192},{33,... | collective-permute-start | bytes 589832 | tf_op jit(solution)/shard_map/while/body/eval_jaxpr/ppermute | solution.py:17
Sparse Core Ops, SparseCore 0:
  12.3 93.9 all-gather.5
  158.6 90.3 all-gather.7
where the time goes:
time: 515 us; the launch traced here: 506 us
  waiting for transfers between devices  222 us (43%)
  other arithmetic  74.1 us (14%)
  matrix products  63 us (12%)
  local copies, waits for them, and re-layouts  46.4 us (9%)
  starting transfers between devices  42.3 us (8%)
  blocking collectives  42.3 us (8%)
  between operations  13.6 us (3%)
    all_gather x2, waiting for transfers between devices, carried_in(): gathered = jax.tree.map(lambda a: lax.all_gather(a, axis), part)  142 us
    ppermute x14, waiting for transfers between devices, passed_along(): lax.ppermute(value, axis, [(source, source + steps) for source in range(l...  79.7 us
    add x62, other arithmetic, linked(): later_part[0][:, None] * earlier[1] + later_part[1]  73.3 us
    dot_general x16, matrix products, propagate(): jnp.dot(matrix, vectors, precision=lax.Precision.HIGHEST, preferred_eleme...  63 us
    all_gather x1, blocking collectives, carried_in(): gathered = jax.tree.map(lambda a: lax.all_gather(a, axis), part)  42.3 us
    ppermute x14, starting transfers between devices, passed_along(): lax.ppermute(value, axis, [(source, source + steps) for source in range(l...  42.2 us
    dynamic_slice x62, local copies, waits for them, and re-layouts, one(): lax.dynamic_index_in_dim(a, source, 0, False)  24.2 us
    while x6, local copies, waits for them, and re-layouts, carried_in(): return lax.fori_loop(0, ahead, one, state)  19.7 us
  transfers between devices with their start and end apart: 16, of which 16 were waited for; matrix products, arithmetic and copies ran while one was open for 0% of the time, Pallas kernels for 0%

commit v1 on v0

v1 whole, which is shorter than its diff:
```python
import functools

import jax
import jax.numpy as jnp
from jax import lax
from jax.experimental import pallas as pl
from jax.experimental.pallas import tpu as pltpu
from jax.sharding import PartitionSpec as P

PASSES = 2
HALVES = 2
DEPTH_CHUNKS = 4

lateral_weight = 0.1
depth_weight = 0.25

MESH = pl.DeviceIdType.MESH
F32 = jnp.float32
BF16 = jnp.bfloat16


def split(x):
    high = x.astype(BF16)
    return high, (x - high.astype(F32)).astype(BF16)


def product(x, high, low):
    rows = x.shape[0]
    x_high, x_low = split(x)
    both = jnp.dot(jnp.concatenate([x_high, x_low], axis=0), high, preferred_element_type=F32)
    return both[:rows] + (both[rows:] + jnp.dot(x_high, low, preferred_element_type=F32))


def kernel(
    layers,
    cells,
    src_hbm,
    rate_hbm,
    lat_hbm,
    down_hbm,
    up_hbm,
    out_ref,
    anchor,
    rate,
    decay,
    stage,
    lat_high,
    lat_low,
    dep_high,
    dep_low,
    fwd_src,
    fwd_rcv,
    car_src,
    car_rcv,
    bwd_src,
    bwd_rcv,
    dec_rcv,
    dec_all,
    cum,
    lefts,
    smooth,
    dep_src,
    dep_rcv,
    load_sem,
    dec_send,
    dec_recv,
    fwd_send,
    fwd_recv,
    car_send,
    car_recv,
    bwd_send,
    bwd_recv,
    dep_send,
    dep_recv,
):
    columns, order = anchor.shape
    group = cells // 2
    ring = group // 2
    width = order // 2
    half_rows = columns // HALVES
    depth_rows = columns // DEPTH_CHUNKS
    block = order // 3

    layer = lax.axis_index("depth")
    cell = lax.axis_index("lat")
    run = cell // group
    here = lax.rem(cell, group)
    z = here // 2
    core = lax.rem(here, 2)
    base = run * group

    loads = [
        pltpu.make_async_copy(src_hbm, anchor, load_sem.at[0]),
        pltpu.make_async_copy(rate_hbm, rate, load_sem.at[1]),
    ]
    for b in range(3):
        rows = pl.ds(b * block, block)
        loads.append(pltpu.make_async_copy(lat_hbm.at[rows], stage.at[0, rows], load_sem.at[2 + b]))
    loads.append(pltpu.make_async_copy(down_hbm, stage.at[1], load_sem.at[5]))
    loads.append(pltpu.make_async_copy(up_hbm, stage.at[2], load_sem.at[6]))
    for load in loads:
        load.start()

    barrier = pltpu.get_barrier_semaphore()
    for offset in range(1, group):
        pl.semaphore_signal(
            barrier, inc=1, device_id=(layer, base + lax.rem(here + offset, group)), device_id_type=MESH
        )
    other_run = (1 - run) * group + here
    pl.semaphore_signal(barrier, inc=1, device_id=(layer, other_run), device_id_type=MESH)

    @pl.when(layer > 0)
    def _():
        pl.semaphore_signal(barrier, inc=1, device_id=(layer - 1, cell), device_id_type=MESH)

    @pl.when(layer < layers - 1)
    def _():
        pl.semaphore_signal(barrier, inc=1, device_id=(layer + 1, cell), device_id_type=MESH)

    def prepare(which, b, high, low):
        rows = pl.ds(b * block, block)
        turned = stage[which, rows, :].T
        top, rest = split(turned)
        high[:, rows] = top
        low[:, rows] = rest

    loads[0].wait()
    for b in range(3):
        rows = pl.ds(b * block, block)
        loads[2 + b].wait()
        prepare(0, b, lat_high, lat_low)
        fwd_src[0, :, rows] = product(anchor[...], lat_high[:, rows], lat_low[:, rows])
    loads[1].wait()
    decay[...] = jnp.exp(-rate[...])

    edges = jnp.where(layer > 0, 1, 0) + jnp.where(layer < layers - 1, 1, 0)
    pl.semaphore_wait(barrier, group + edges)

    offsets = [ring // 2]
    for step in range(ring // 2 - 1, 0, -1):
        offsets += [step, ring - step]

    def piece(owner_z, half):
        return (
            pl.ds(pl.multiple_of(half * half_rows + 8 * (owner_z // 2), 8), 8),
            pl.ds(pl.multiple_of(lax.rem(owner_z, 2) * width, width), width),
        )

    def forward_copy(turn, half, owner_z):
        rows, modes = piece(owner_z, half)
        owner = owner_z * 2 + half
        return pltpu.make_async_remote_copy(
            src_ref=fwd_src.at[turn, rows, modes],
            dst_ref=fwd_rcv.at[turn, here],
            send_sem=fwd_send.at[turn, owner],
            recv_sem=fwd_recv.at[turn, here],
            device_id=(layer, base + owner),
            device_id_type=MESH,
        )

    def forward_own(turn):
        rows, modes = piece(z, core)
        return pltpu.make_async_copy(
            fwd_src.at[turn, rows, modes], fwd_rcv.at[turn, here], fwd_recv.at[turn, here]
        )

    def send_forward(turn, half):
        for offset in offsets:
            forward_copy(turn, half, lax.rem(z + offset, ring)).start()

        @pl.when(core != half)
        def _():
            forward_copy(turn, half, z).start()

        @pl.when(core == half)
        def _():
            forward_own(turn).start()

    def decay_copy(owner_z, half):
        owner = owner_z * 2 + half
        _, modes = piece(owner_z, half)
        return pltpu.make_async_remote_copy(
            src_ref=decay.at[:, modes],
            dst_ref=dec_rcv.at[here],
            send_sem=dec_send.at[owner],
            recv_sem=dec_recv.at[here],
            device_id=(layer, base + owner),
            device_id_type=MESH,
        )

    def decay_own():
        _, modes = piece(z, core)
        return pltpu.make_async_copy(decay.at[:, modes], dec_rcv.at[here], dec_recv.at[here])

    def all_peers(action):
        for half in range(HALVES):
            for offset in offsets:
                action(lax.rem(z + offset, ring), half)
        action(z, 1 - core)

    for half in range(HALVES):
        send_forward(0, half)
    all_peers(lambda owner_z, half: decay_copy(owner_z, half).start())
    decay_own().start()

    def carry_copy(turn):
        return pltpu.make_async_remote_copy(
            src_ref=car_src.at[turn],
            dst_ref=car_rcv.at[turn],
            send_sem=car_send.at[turn],
            recv_sem=car_recv.at[turn],
            device_id=(layer, other_run),
            device_id_type=MESH,
        )

    def backward_copy(turn, target):
        rows, modes = piece(z, core)
        return pltpu.make_async_remote_copy(
            src_ref=bwd_src.at[turn, target],
            dst_ref=bwd_rcv.at[turn, rows, modes],
            send_sem=bwd_send.at[turn, target],
            recv_sem=bwd_recv.at[turn, here],
            device_id=(layer, base + target),
            device_id_type=MESH,
        )

    def backward_own(turn):
        rows, modes = piece(z, core)
        return pltpu.make_async_copy(
            bwd_src.at[turn, here], bwd_rcv.at[turn, rows, modes], bwd_recv.at[turn, here]
        )

    def damping():
        for j in range(group):
            pltpu.make_async_copy(dec_rcv.at[j], dec_rcv.at[j], dec_recv.at[j]).wait()
        for j in range(group):
            dec_all[j] = jnp.broadcast_to(dec_rcv[j], (8, width))
        right = jnp.ones((8, width), F32)
        for j in range(group):
            right = right * dec_all[j]
            cum[j] = right
        left = jnp.ones((8, width), F32)
        for j in range(group - 1, -1, -1):
            left = left * dec_all[j]
            cum[j] = jnp.where(run == 1, cum[j], left)

    def own_sweep(turn):
        for j in range(group):
            pltpu.make_async_copy(fwd_rcv.at[turn, j], fwd_rcv.at[turn, j], fwd_recv.at[turn, j]).wait()
        right = jnp.zeros((8, width), F32)
        left = jnp.zeros((8, width), F32)
        for j in range(group):
            right = dec_all[j] * right + fwd_rcv[turn, j]
            bwd_src[turn, j] = right
            back = group - 1 - j
            left = dec_all[back] * left + fwd_rcv[turn, back]
            lefts[back] = left
        car_src[turn] = jnp.where(run == 0, right, left)
        carry_copy(turn).start()
        carry_copy(turn).wait_recv()
        carry = car_rcv[turn]
        for j in range(group):
            bwd_src[turn, j] = bwd_src[turn, j] + lefts[j] + cum[j] * carry
        for core_to in range(2):
            for offset in offsets:
                backward_copy(turn, lax.rem(z + offset, ring) * 2 + core_to).start()
        backward_copy(turn, z * 2 + 1 - core).start()
        backward_own(turn).start()

    def collected(turn, half):
        for owner_z in range(ring):
            rows, modes = piece(owner_z, half)
            ref = bwd_rcv.at[turn, rows, modes]
            pltpu.make_async_copy(ref, ref, bwd_recv.at[turn, owner_z * 2 + half]).wait()
        rows = pl.ds(half * half_rows, half_rows)
        return anchor[rows, :] + lateral_weight * bwd_rcv[turn, rows, :]

    loads[5].wait()
    for b in range(3):
        prepare(1, b, dep_high.at[0], dep_low.at[0])
    damping()
    own_sweep(0)
    loads[6].wait()
    for b in range(3):
        prepare(2, b, dep_high.at[1], dep_low.at[1])
    for half in range(HALVES):
        rows = pl.ds(half * half_rows, half_rows)
        fwd_src[1, rows, :] = product(collected(0, half), lat_high[...], lat_low[...])
        send_forward(1, half)
    own_sweep(1)

    first = jnp.where(layer >= layers // 2, 1, 0)
    second = 1 - first
    place = jnp.where(first == 0, layer, layers - 1 - layer)

    def chunk_rows(k):
        return pl.ds(pl.multiple_of(k * depth_rows, 8), depth_rows)

    def depth_copy(source, way, k):
        rows = chunk_rows(k)
        return pltpu.make_async_remote_copy(
            src_ref=source.at[rows],
            dst_ref=dep_rcv.at[way, rows],
            send_sem=dep_send.at[way, k],
            recv_sem=dep_recv.at[way, k],
            device_id=(layer + 1 - 2 * way, cell),
            device_id_type=MESH,
        )

    def arrived(way, k):
        ref = dep_rcv.at[way, chunk_rows(k)]
        pltpu.make_async_copy(ref, ref, dep_recv.at[way, k]).wait()

    for half in range(HALVES):
        rows = pl.ds(half * half_rows, half_rows)
        smooth[rows, :] = collected(1, half)

        @pl.when(place == 0)
        def _():
            for k in range(half * DEPTH_CHUNKS // HALVES, (half + 1) * DEPTH_CHUNKS // HALVES):
                depth_copy(smooth, first, k).start()

    def step(way, k):
        rows = chunk_rows(k)
        arrived(way, k)
        dep_src[way, rows, :] = smooth[rows, :] + product(
            dep_rcv[way, rows, :], dep_high[way], dep_low[way]
        )
        depth_copy(dep_src.at[way], way, k).start()

    @pl.when(place > 0)
    def _():
        @pl.loop(0, DEPTH_CHUNKS)
        def _(k):
            step(first, k)

        out_ref[...] = smooth[...] + depth_weight * dep_rcv[first]

    @pl.when(place == 0)
    def _():
        out_ref[...] = smooth[...]

        @pl.loop(0, DEPTH_CHUNKS)
        def _(k):
            arrived(second, k)

    @pl.when(place > 0)
    def _():
        @pl.loop(0, DEPTH_CHUNKS)
        def _(k):
            step(second, k)

    out_ref[...] = out_ref[...] + depth_weight * dep_rcv[second]

    for turn in range(PASSES):
        for half in range(HALVES):
            for offset in offsets:
                owner_z = lax.rem(z + offset, ring)
                forward_copy(turn, half, owner_z).wait_send()
                backward_copy(turn, owner_z * 2 + half).wait_send()
        forward_copy(turn, 1 - core, z).wait_send()
        backward_copy(turn, z * 2 + 1 - core).wait_send()
        carry_copy(turn).wait_send()
    all_peers(lambda owner_z, half: decay_copy(owner_z, half).wait_send())
    for k in range(DEPTH_CHUNKS):
        depth_copy(smooth, first, k).wait_send()

        @pl.when(place > 0)
        def _():
            depth_copy(smooth, second, k).wait_send()


def shards(source, rate, lat_op, down_op, up_op):
    order, columns = source.shape[2:]
    layers = lax.axis_size("depth")
    cells = lax.axis_size("lat")
    group = cells // 2
    width = order // 2
    any_space = pl.BlockSpec(memory_space=pl.ANY)
    vmem = pltpu.VMEM
    dma = pltpu.SemaphoreType.DMA
    traces = pl.pallas_call(
        functools.partial(kernel, layers, cells),
        name="sweeps",
        out_shape=jax.ShapeDtypeStruct((columns, order), F32),
        in_specs=[any_space] * 5,
        out_specs=pl.BlockSpec(memory_space=pltpu.VMEM),
        scratch_shapes=[
            vmem((columns, order), F32),
            vmem((1, order), F32),
            vmem((1, order), F32),
            vmem((3, order, order), F32),
            vmem((order, order), BF16),
            vmem((order, order), BF16),
            vmem((2, order, order), BF16),
            vmem((2, order, order), BF16),
            vmem((PASSES, columns, order), F32),
            vmem((PASSES, group, 8, width), F32),
            vmem((PASSES, 8, width), F32),
            vmem((PASSES, 8, width), F32),
            vmem((PASSES, group, 8, width), F32),
            vmem((PASSES, columns, order), F32),
            vmem((group, 1, width), F32),
            vmem((group, 8, width), F32),
            vmem((group, 8, width), F32),
            vmem((group, 8, width), F32),
            vmem((columns, order), F32),
            vmem((2, columns, order), F32),
            vmem((2, columns, order), F32),
            dma((7,)),
            dma((group,)),
            dma((group,)),
            dma((PASSES, group)),
            dma((PASSES, group)),
            dma((PASSES,)),
            dma((PASSES,)),
            dma((PASSES, group)),
            dma((PASSES, group)),
            dma((2, DEPTH_CHUNKS)),
            dma((2, DEPTH_CHUNKS)),
        ],
        compiler_params=pltpu.CompilerParams(
            collective_id=0, has_side_effects=True, vmem_limit_bytes=60 << 20
        ),
    )(
        source.reshape(order, columns).T,
        rate.reshape(1, order),
        lat_op.reshape(order, order),
        down_op.reshape(order, order),
        up_op.reshape(order, order),
    )
    return traces.T.reshape(1, 1, order, columns)


def solution(mesh):
    spec = P("depth", "lat", None, None)
    in_specs = (spec, P("depth", "lat", None), spec, spec, spec)
    return jax.shard_map(shards, mesh=mesh, in_specs=in_specs, out_specs=spec, check_vma=False)
```

time: 515 us -> 79.3 us (0.15); the launches traced: 506 us -> 79.2 us
  waiting for transfers between devices: 222 us -> 0 us
  Pallas kernels: 0 us -> 77.6 us
  other arithmetic: 74.1 us -> 0 us
  matrix products: 63 us -> 0 us
  local copies, waits for them, and re-layouts: 46.4 us -> 1.62 us
  blocking collectives: 42.3 us -> 0 us
  starting transfers between devices: 42.3 us -> 0 us
  between operations: 13.6 us -> 0.01 us
    all_gather x2 -> x0, waiting for transfers between devices: 142 us -> none  [carried_in(): gathered = jax.tree.map(lambda a: lax.all_gather(a, axis), part)]
    ppermute x14 -> x0, waiting for transfers between devices: 79.7 us -> none  [passed_along(): lax.ppermute(value, axis, [(source, source + steps) for source in range(l...]
    pallas_call x0 -> x1, Pallas kernels: none -> 77.6 us  [shards(): pl.pallas_call(functools.partial(kernel, layers, cells), name='sweeps', o...]
    add x63 -> x0, other arithmetic: 73.4 us -> none  [the longest x62 73.3 us: linked(): later_part[0][:, None] * earlier[1] + later_part[1]]
    dot_general x16 -> x0, matrix products: 63 us -> none  [propagate(): jnp.dot(matrix, vectors, precision=lax.Precision.HIGHEST, preferred_eleme...]
    all_gather x1 -> x0, blocking collectives: 42.3 us -> none  [carried_in(): gathered = jax.tree.map(lambda a: lax.all_gather(a, axis), part)]
    ppermute x14 -> x0, starting transfers between devices: 42.2 us -> none  [passed_along(): lax.ppermute(value, axis, [(source, source + steps) for source in range(l...]
    dynamic_slice x62 -> x0, local copies, waits for them, and re-layouts: 24.2 us -> none  [one(): lax.dynamic_index_in_dim(a, source, 0, False)]
  transfers between devices with their start and end apart: 16 -> 0, of which waited for: 16 -> 0; matrix products, arithmetic and copies ran while one was open for 0% -> 0% of each run, Pallas kernels for 0% -> 0%
where the time goes in v1:
time: 79.3 us; the launch traced here: 79.2 us
  Pallas kernels  77.6 us (98%)
  local copies, waits for them, and re-layouts  1.62 us (2%)
    pallas_call x1, Pallas kernels, shards(): pl.pallas_call(functools.partial(kernel, layers, cells), name='sweeps', o...  77.6 us
    unnamed x1, local copies, waits for them, and re-layouts  1.62 us

profile of v1, /device:TPU:16, one launch (start us, length us, event | category | flops | bytes accessed | tf_op | source)
XLA Modules:
  0.0 79.2 jit_solution(11131244201639281196)
XLA Ops:
  0.0 77.6 %sweeps.1 = f32[64,768]{1,0:T(8,128)} custom-call(f32[64,768]{1,0:T(8,128)} %bitcast.14, f32[1,768]{1,0:T(1,128)} %bitcast.15, f32[768,768]{1,0:T(8,128)} %bitcast.10, f32[768,768]{1,0:T(8,128)} %bitcast.11, f32[768,768]{1,0:T(8,128)} %bitcast.12), custom_call_target="tpu_custom_call" | custom-call | tf_op jit(solution)/shard_map/sweeps/pallas_call | solution.py:382
  77.6 1.6 %copy.7 = f32[1,1,768,64]{2,3,1,0:T(8,128)} copy(f32[1,1,768,64]{2,3,1,0:T(8,128)} %bitcast.13) | data formatting | bytes 393216

commit v2 on v1

--- a/solution.py
+++ b/solution.py
@@ -8,8 +8,8 @@
 from jax.sharding import PartitionSpec as P
 
 PASSES = 2
-HALVES = 2
-DEPTH_CHUNKS = 4
+CHUNKS = 2
+DEPTH_CHUNKS = 8
 
 lateral_weight = 0.1
 depth_weight = 0.25
@@ -75,18 +75,19 @@
 ):
     columns, order = anchor.shape
     group = cells // 2
-    ring = group // 2
     width = order // 2
-    half_rows = columns // HALVES
+    chunk = columns // CHUNKS
+    owners = group // CHUNKS
     depth_rows = columns // DEPTH_CHUNKS
+    per_chunk = DEPTH_CHUNKS // CHUNKS
     block = order // 3
 
     layer = lax.axis_index("depth")
     cell = lax.axis_index("lat")
     run = cell // group
     here = lax.rem(cell, group)
-    z = here // 2
-    core = lax.rem(here, 2)
+    place_in_chunk = here // CHUNKS
+    own_chunk = lax.rem(here, CHUNKS)
     base = run * group
 
     loads = [
@@ -98,7 +99,7 @@
         loads.append(pltpu.make_async_copy(lat_hbm.at[rows], stage.at[0, rows], load_sem.at[2 + b]))
     loads.append(pltpu.make_async_copy(down_hbm, stage.at[1], load_sem.at[5]))
     loads.append(pltpu.make_async_copy(up_hbm, stage.at[2], load_sem.at[6]))
-    for load in loads:
+    for load in loads[:5]:
         load.start()
 
     barrier = pltpu.get_barrier_semaphore()
@@ -130,27 +131,27 @@
         loads[2 + b].wait()
         prepare(0, b, lat_high, lat_low)
         fwd_src[0, :, rows] = product(anchor[...], lat_high[:, rows], lat_low[:, rows])
+    for load in loads[5:]:
+        load.start()
     loads[1].wait()
     decay[...] = jnp.exp(-rate[...])
 
     edges = jnp.where(layer > 0, 1, 0) + jnp.where(layer < layers - 1, 1, 0)
     pl.semaphore_wait(barrier, group + edges)
 
-    offsets = [ring // 2]
-    for step in range(ring // 2 - 1, 0, -1):
-        offsets += [step, ring - step]
-
-    def piece(owner_z, half):
+    def far_first(count):
+        return sorted(range(1, count), key=lambda step: -min(step, count - step))
+
+    def piece(owner):
+        part = owner // CHUNKS
         return (
-            pl.ds(pl.multiple_of(half * half_rows + 8 * (owner_z // 2), 8), 8),
-            pl.ds(pl.multiple_of(lax.rem(owner_z, 2) * width, width), width),
-        )
-
-    def forward_copy(turn, half, owner_z):
-        rows, modes = piece(owner_z, half)
-        owner = owner_z * 2 + half
+            pl.ds(pl.multiple_of(lax.rem(owner, CHUNKS) * chunk + 8 * (part // 2), 8), 8),
+            pl.ds(pl.multiple_of(lax.rem(part, 2) * width, width), width),
+        )
+
+    def forward_copy(turn, owner):
         return pltpu.make_async_remote_copy(
-            src_ref=fwd_src.at[turn, rows, modes],
+            src_ref=fwd_src.at[turn, *piece(owner)],
             dst_ref=fwd_rcv.at[turn, here],
             send_sem=fwd_send.at[turn, owner],
             recv_sem=fwd_recv.at[turn, here],
@@ -159,28 +160,13 @@
         )
 
     def forward_own(turn):
-        rows, modes = piece(z, core)
         return pltpu.make_async_copy(
-            fwd_src.at[turn, rows, modes], fwd_rcv.at[turn, here], fwd_recv.at[turn, here]
-        )
-
-    def send_forward(turn, half):
-        for offset in offsets:
-            forward_copy(turn, half, lax.rem(z + offset, ring)).start()
-
-        @pl.when(core != half)
-        def _():
-            forward_copy(turn, half, z).start()
-
-        @pl.when(core == half)
-        def _():
-            forward_own(turn).start()
-
-    def decay_copy(owner_z, half):
-        owner = owner_z * 2 + half
-        _, modes = piece(owner_z, half)
+            fwd_src.at[turn, *piece(here)], fwd_rcv.at[turn, here], fwd_recv.at[turn, here]
+        )
+
+    def decay_copy(owner):
         return pltpu.make_async_remote_copy(
-            src_ref=decay.at[:, modes],
+            src_ref=decay.at[:, piece(owner)[1]],
             dst_ref=dec_rcv.at[here],
             send_sem=dec_send.at[owner],
             recv_sem=dec_recv.at[here],
@@ -189,19 +175,31 @@
         )
 
     def decay_own():
-        _, modes = piece(z, core)
-        return pltpu.make_async_copy(decay.at[:, modes], dec_rcv.at[here], dec_recv.at[here])
-
-    def all_peers(action):
-        for half in range(HALVES):
-            for offset in offsets:
-                action(lax.rem(z + offset, ring), half)
-        action(z, 1 - core)
-
-    for half in range(HALVES):
-        send_forward(0, half)
-    all_peers(lambda owner_z, half: decay_copy(owner_z, half).start())
-    decay_own().start()
+        return pltpu.make_async_copy(decay.at[:, piece(here)[1]], dec_rcv.at[here], dec_recv.at[here])
+
+    def owner_of(index, offset):
+        return index + CHUNKS * lax.rem(place_in_chunk + offset, owners)
+
+    def send_forward(turn, index):
+        for offset in far_first(owners):
+            if turn == 0:
+                decay_copy(owner_of(index, offset)).start()
+            forward_copy(turn, owner_of(index, offset)).start()
+
+        @pl.when(own_chunk != index)
+        def _():
+            if turn == 0:
+                decay_copy(owner_of(index, 0)).start()
+            forward_copy(turn, owner_of(index, 0)).start()
+
+        @pl.when(own_chunk == index)
+        def _():
+            if turn == 0:
+                decay_own().start()
+            forward_own(turn).start()
+
+    for index in range(CHUNKS):
+        send_forward(0, index)
 
     def carry_copy(turn):
         return pltpu.make_async_remote_copy(
@@ -214,10 +212,9 @@
         )
 
     def backward_copy(turn, target):
-        rows, modes = piece(z, core)
         return pltpu.make_async_remote_copy(
             src_ref=bwd_src.at[turn, target],
-            dst_ref=bwd_rcv.at[turn, rows, modes],
+            dst_ref=bwd_rcv.at[turn, *piece(here)],
             send_sem=bwd_send.at[turn, target],
             recv_sem=bwd_recv.at[turn, here],
             device_id=(layer, base + target),
@@ -225,10 +222,12 @@
         )
 
     def backward_own(turn):
-        rows, modes = piece(z, core)
         return pltpu.make_async_copy(
-            bwd_src.at[turn, here], bwd_rcv.at[turn, rows, modes], bwd_recv.at[turn, here]
-        )
+            bwd_src.at[turn, here], bwd_rcv.at[turn, *piece(here)], bwd_recv.at[turn, here]
+        )
+
+    def peer(offset):
+        return lax.rem(here + offset, group)
 
     def damping():
         for j in range(group):
@@ -244,7 +243,7 @@
             left = left * dec_all[j]
             cum[j] = jnp.where(run == 1, cum[j], left)
 
-    def own_sweep(turn):
+    def own_sweep(turn, meanwhile):
         for j in range(group):
             pltpu.make_async_copy(fwd_rcv.at[turn, j], fwd_rcv.at[turn, j], fwd_recv.at[turn, j]).wait()
         right = jnp.zeros((8, width), F32)
@@ -257,47 +256,54 @@
             lefts[back] = left
         car_src[turn] = jnp.where(run == 0, right, left)
         carry_copy(turn).start()
+        meanwhile()
         carry_copy(turn).wait_recv()
         carry = car_rcv[turn]
         for j in range(group):
             bwd_src[turn, j] = bwd_src[turn, j] + lefts[j] + cum[j] * carry
-        for core_to in range(2):
-            for offset in offsets:
-                backward_copy(turn, lax.rem(z + offset, ring) * 2 + core_to).start()
-        backward_copy(turn, z * 2 + 1 - core).start()
+        for offset in far_first(group):
+            backward_copy(turn, peer(offset)).start()
         backward_own(turn).start()
 
-    def collected(turn, half):
-        for owner_z in range(ring):
-            rows, modes = piece(owner_z, half)
-            ref = bwd_rcv.at[turn, rows, modes]
-            pltpu.make_async_copy(ref, ref, bwd_recv.at[turn, owner_z * 2 + half]).wait()
-        rows = pl.ds(half * half_rows, half_rows)
+    def chunk_rows(index):
+        return pl.ds(index * chunk, chunk)
+
+    def collected(turn, index):
+        for part in range(owners):
+            owner = index + CHUNKS * part
+            ref = bwd_rcv.at[turn, *piece(owner)]
+            pltpu.make_async_copy(ref, ref, bwd_recv.at[turn, owner]).wait()
+        rows = chunk_rows(index)
         return anchor[rows, :] + lateral_weight * bwd_rcv[turn, rows, :]
 
-    loads[5].wait()
-    for b in range(3):
-        prepare(1, b, dep_high.at[0], dep_low.at[0])
+    def prepare_down():
+        loads[5].wait()
+        for b in range(3):
+            prepare(1, b, dep_high.at[0], dep_low.at[0])
+
+    def prepare_up():
+        loads[6].wait()
+        for b in range(3):
+            prepare(2, b, dep_high.at[1], dep_low.at[1])
+
+    prepare_down()
     damping()
-    own_sweep(0)
-    loads[6].wait()
-    for b in range(3):
-        prepare(2, b, dep_high.at[1], dep_low.at[1])
-    for half in range(HALVES):
-        rows = pl.ds(half * half_rows, half_rows)
-        fwd_src[1, rows, :] = product(collected(0, half), lat_high[...], lat_low[...])
-        send_forward(1, half)
-    own_sweep(1)
+    own_sweep(0, prepare_up)
+    for index in range(CHUNKS):
+        rows = chunk_rows(index)
+        fwd_src[1, rows, :] = product(collected(0, index), lat_high[...], lat_low[...])
+        send_forward(1, index)
+    own_sweep(1, lambda: None)
 
     first = jnp.where(layer >= layers // 2, 1, 0)
     second = 1 - first
     place = jnp.where(first == 0, layer, layers - 1 - layer)
 
-    def chunk_rows(k):
+    def depth_chunk(k):
         return pl.ds(pl.multiple_of(k * depth_rows, 8), depth_rows)
 
     def depth_copy(source, way, k):
-        rows = chunk_rows(k)
+        rows = depth_chunk(k)
         return pltpu.make_async_remote_copy(
             src_ref=source.at[rows],
             dst_ref=dep_rcv.at[way, rows],
@@ -308,60 +314,55 @@
         )
 
     def arrived(way, k):
-        ref = dep_rcv.at[way, chunk_rows(k)]
+        ref = dep_rcv.at[way, depth_chunk(k)]
         pltpu.make_async_copy(ref, ref, dep_recv.at[way, k]).wait()
 
-    for half in range(HALVES):
-        rows = pl.ds(half * half_rows, half_rows)
-        smooth[rows, :] = collected(1, half)
-
-        @pl.when(place == 0)
-        def _():
-            for k in range(half * DEPTH_CHUNKS // HALVES, (half + 1) * DEPTH_CHUNKS // HALVES):
-                depth_copy(smooth, first, k).start()
-
     def step(way, k):
-        rows = chunk_rows(k)
+        rows = depth_chunk(k)
         arrived(way, k)
         dep_src[way, rows, :] = smooth[rows, :] + product(
             dep_rcv[way, rows, :], dep_high[way], dep_low[way]
         )
         depth_copy(dep_src.at[way], way, k).start()
 
-    @pl.when(place > 0)
-    def _():
-        @pl.loop(0, DEPTH_CHUNKS)
-        def _(k):
-            step(first, k)
-
-        out_ref[...] = smooth[...] + depth_weight * dep_rcv[first]
-
-    @pl.when(place == 0)
-    def _():
-        out_ref[...] = smooth[...]
-
-        @pl.loop(0, DEPTH_CHUNKS)
-        def _(k):
+    for index in range(CHUNKS):
+        rows = chunk_rows(index)
+        smooth[rows, :] = collected(1, index)
+
+        @pl.when(place == 0)
+        def _():
+            for k in range(index * per_chunk, (index + 1) * per_chunk):
+                depth_copy(smooth, first, k).start()
+            out_ref[rows, :] = smooth[rows, :]
+
+        @pl.when(place > 0)
+        def _():
+            @pl.loop(index * per_chunk, (index + 1) * per_chunk)
+            def _(k):
+                step(first, k)
+
+            out_ref[rows, :] = smooth[rows, :] + depth_weight * dep_rcv[first, rows, :]
+
+    @pl.loop(0, DEPTH_CHUNKS)
+    def _(k):
+        @pl.when(place == 0)
+        def _():
             arrived(second, k)
 
-    @pl.when(place > 0)
-    def _():
-        @pl.loop(0, DEPTH_CHUNKS)
-        def _(k):
+        @pl.when(place > 0)
+        def _():
             step(second, k)
 
-    out_ref[...] = out_ref[...] + depth_weight * dep_rcv[second]
-
+        rows = depth_chunk(k)
+        out_ref[rows, :] = out_ref[rows, :] + depth_weight * dep_rcv[second, rows, :]
+
+    for offset in range(1, group):
+        for turn in range(PASSES):
+            forward_copy(turn, peer(offset)).wait_send()
+            backward_copy(turn, peer(offset)).wait_send()
+        decay_copy(peer(offset)).wait_send()
     for turn in range(PASSES):
-        for half in range(HALVES):
-            for offset in offsets:
-                owner_z = lax.rem(z + offset, ring)
-                forward_copy(turn, half, owner_z).wait_send()
-                backward_copy(turn, owner_z * 2 + half).wait_send()
-        forward_copy(turn, 1 - core, z).wait_send()
-        backward_copy(turn, z * 2 + 1 - core).wait_send()
         carry_copy(turn).wait_send()
-    all_peers(lambda owner_z, half: decay_copy(owner_z, half).wait_send())
     for k in range(DEPTH_CHUNKS):
         depth_copy(smooth, first, k).wait_send()
 

time: 79.3 us -> 75.4 us (0.951)
  Pallas kernels: 77.6 us -> 73.4 us
    pallas_call x1, Pallas kernels: 77.6 us -> 73.4 us  [shards(): pl.pallas_call(functools.partial(kernel, layers, cells), name='sweeps', o...]
where the time goes in v2:
time: 75.4 us; the launch traced here: 75 us
  Pallas kernels  73.4 us (97%)
  local copies, waits for them, and re-layouts  1.62 us (2%)
    pallas_call x1, Pallas kernels, shards(): pl.pallas_call(functools.partial(kernel, layers, cells), name='sweeps', o...  73.4 us
    unnamed x1, local copies, waits for them, and re-layouts  1.62 us

profile of v2, /device:TPU:16, one launch (start us, length us, event | category | flops | bytes accessed | tf_op | source)
XLA Modules:
  0.0 75.0 jit_solution(6659319106853668187)
XLA Ops:
  0.0 73.4 %sweeps.1 = f32[64,768]{1,0:T(8,128)} custom-call(f32[64,768]{1,0:T(8,128)} %bitcast.14, f32[1,768]{1,0:T(1,128)} %bitcast.15, f32[768,768]{1,0:T(8,128)} %bitcast.10, f32[768,768]{1,0:T(8,128)} %bitcast.11, f32[768,768]{1,0:T(8,128)} %bitcast.12), custom_call_target="tpu_custom_call" | custom-call | tf_op jit(solution)/shard_map/sweeps/pallas_call | solution.py:383
  73.4 1.6 %copy.7 = f32[1,1,768,64]{2,3,1,0:T(8,128)} copy(f32[1,1,768,64]{2,3,1,0:T(8,128)} %bitcast.13) | data formatting | bytes 393216

commit v3 on v2

--- a/solution.py
+++ b/solution.py
@@ -9,7 +9,9 @@
 
 PASSES = 2
 CHUNKS = 2
-DEPTH_CHUNKS = 8
+DEPTH_CHUNKS = 4
+PARTS = 12
+RELAYED = (1, 5, 6, 10, 11)
 
 lateral_weight = 0.1
 depth_weight = 0.25
@@ -61,6 +63,8 @@
     smooth,
     dep_src,
     dep_rcv,
+    mate,
+    relay,
     load_sem,
     dec_send,
     dec_recv,
@@ -72,6 +76,11 @@
     bwd_recv,
     dep_send,
     dep_recv,
+    mate_send,
+    mate_recv,
+    part_send,
+    part_recv,
+    relay_recv,
 ):
     columns, order = anchor.shape
     group = cells // 2
@@ -81,6 +90,7 @@
     depth_rows = columns // DEPTH_CHUNKS
     per_chunk = DEPTH_CHUNKS // CHUNKS
     block = order // 3
+    part_rows = order // PARTS
 
     layer = lax.axis_index("depth")
     cell = lax.axis_index("lat")
@@ -90,6 +100,32 @@
     own_chunk = lax.rem(here, CHUNKS)
     base = run * group
 
+    way = jnp.where(jnp.logical_or(layer == 3, layer >= 5), 1, 0)
+    rank = jnp.where(way == 0, layer, layers - 1 - layer)
+    inner = rank >= 2
+    neighbour = layer + 1 - 2 * lax.rem(layer, 2)
+    quad = (layer // 4) * 4
+    across = jnp.where(layer < 4, layer + 2, layer - 2)
+    relay_by = jnp.where(layer < 4, 3 - layer, 11 - layer)
+    after = rank + jnp.where(rank < 2, 1, 2)
+    chain_to = jnp.where(way == 0, after, layers - 1 - after)
+    chain_slot = jnp.where(rank == 4, 1, 0)
+    back_to = layer - 1 + 2 * way
+
+    def operator_load(own, slot):
+        return pltpu.make_async_copy(own, stage.at[slot], load_sem.at[4 + slot])
+
+    def load_operators():
+        for turn, (main, other) in enumerate(((down_hbm, up_hbm), (up_hbm, down_hbm))):
+
+            @pl.when(jnp.logical_and(way == turn, rank > 0))
+            def _():
+                operator_load(main, 1).start()
+
+            @pl.when(jnp.logical_and(way == turn, rank == 1))
+            def _():
+                operator_load(other, 2).start()
+
     loads = [
         pltpu.make_async_copy(src_hbm, anchor, load_sem.at[0]),
         pltpu.make_async_copy(rate_hbm, rate, load_sem.at[1]),
@@ -97,9 +133,7 @@
     for b in range(3):
         rows = pl.ds(b * block, block)
         loads.append(pltpu.make_async_copy(lat_hbm.at[rows], stage.at[0, rows], load_sem.at[2 + b]))
-    loads.append(pltpu.make_async_copy(down_hbm, stage.at[1], load_sem.at[5]))
-    loads.append(pltpu.make_async_copy(up_hbm, stage.at[2], load_sem.at[6]))
-    for load in loads[:5]:
+    for load in loads:
         load.start()
 
     barrier = pltpu.get_barrier_semaphore()
@@ -110,13 +144,13 @@
     other_run = (1 - run) * group + here
     pl.semaphore_signal(barrier, inc=1, device_id=(layer, other_run), device_id_type=MESH)
 
-    @pl.when(layer > 0)
-    def _():
-        pl.semaphore_signal(barrier, inc=1, device_id=(layer - 1, cell), device_id_type=MESH)
-
-    @pl.when(layer < layers - 1)
-    def _():
-        pl.semaphore_signal(barrier, inc=1, device_id=(layer + 1, cell), device_id_type=MESH)
+    for offset in range(1, 4):
+        mate_layer = quad + lax.rem(layer - quad + offset, 4)
+        pl.semaphore_signal(barrier, inc=1, device_id=(mate_layer, cell), device_id_type=MESH)
+
+    @pl.when(inner)
+    def _():
+        pl.semaphore_signal(barrier, inc=1, device_id=(across, cell), device_id_type=MESH)
 
     def prepare(which, b, high, low):
         rows = pl.ds(b * block, block)
@@ -131,13 +165,11 @@
         loads[2 + b].wait()
         prepare(0, b, lat_high, lat_low)
         fwd_src[0, :, rows] = product(anchor[...], lat_high[:, rows], lat_low[:, rows])
-    for load in loads[5:]:
-        load.start()
+    load_operators()
     loads[1].wait()
     decay[...] = jnp.exp(-rate[...])
 
-    edges = jnp.where(layer > 0, 1, 0) + jnp.where(layer < layers - 1, 1, 0)
-    pl.semaphore_wait(barrier, group + edges)
+    pl.semaphore_wait(barrier, group + 3 + jnp.where(inner, 1, 0))
 
     def far_first(count):
         return sorted(range(1, count), key=lambda step: -min(step, count - step))
@@ -153,29 +185,29 @@
         return pltpu.make_async_remote_copy(
             src_ref=fwd_src.at[turn, *piece(owner)],
             dst_ref=fwd_rcv.at[turn, here],
-            send_sem=fwd_send.at[turn, owner],
-            recv_sem=fwd_recv.at[turn, here],
+            send_sem=fwd_send.at[turn],
+            recv_sem=fwd_recv.at[turn],
             device_id=(layer, base + owner),
             device_id_type=MESH,
         )
 
     def forward_own(turn):
         return pltpu.make_async_copy(
-            fwd_src.at[turn, *piece(here)], fwd_rcv.at[turn, here], fwd_recv.at[turn, here]
+            fwd_src.at[turn, *piece(here)], fwd_rcv.at[turn, here], fwd_recv.at[turn]
         )
 
     def decay_copy(owner):
         return pltpu.make_async_remote_copy(
             src_ref=decay.at[:, piece(owner)[1]],
             dst_ref=dec_rcv.at[here],
-            send_sem=dec_send.at[owner],
-            recv_sem=dec_recv.at[here],
+            send_sem=dec_send,
+            recv_sem=dec_recv,
             device_id=(layer, base + owner),
             device_id_type=MESH,
         )
 
     def decay_own():
-        return pltpu.make_async_copy(decay.at[:, piece(here)[1]], dec_rcv.at[here], dec_recv.at[here])
+        return pltpu.make_async_copy(decay.at[:, piece(here)[1]], dec_rcv.at[here], dec_recv)
 
     def owner_of(index, offset):
         return index + CHUNKS * lax.rem(place_in_chunk + offset, owners)
@@ -215,23 +247,25 @@
         return pltpu.make_async_remote_copy(
             src_ref=bwd_src.at[turn, target],
             dst_ref=bwd_rcv.at[turn, *piece(here)],
-            send_sem=bwd_send.at[turn, target],
-            recv_sem=bwd_recv.at[turn, here],
+            send_sem=bwd_send.at[turn],
+            recv_sem=bwd_recv.at[turn, own_chunk],
             device_id=(layer, base + target),
             device_id_type=MESH,
         )
 
     def backward_own(turn):
         return pltpu.make_async_copy(
-            bwd_src.at[turn, here], bwd_rcv.at[turn, *piece(here)], bwd_recv.at[turn, here]
+            bwd_src.at[turn, here], bwd_rcv.at[turn, *piece(here)], bwd_recv.at[turn, own_chunk]
         )
 
     def peer(offset):
         return lax.rem(here + offset, group)
 
+    def all_of(ref, sem):
+        pltpu.make_async_copy(ref, ref, sem).wait()
+
     def damping():
-        for j in range(group):
-            pltpu.make_async_copy(dec_rcv.at[j], dec_rcv.at[j], dec_recv.at[j]).wait()
+        all_of(dec_rcv, dec_recv)
         for j in range(group):
             dec_all[j] = jnp.broadcast_to(dec_rcv[j], (8, width))
         right = jnp.ones((8, width), F32)
@@ -243,9 +277,50 @@
             left = left * dec_all[j]
             cum[j] = jnp.where(run == 1, cum[j], left)
 
+    def part(b):
+        return pl.ds(b * part_rows, part_rows)
+
+    def third(b):
+        return 3 * b // PARTS
+
+    def relay_part(b):
+        return relay.at[part(RELAYED.index(b))]
+
+    def ship_copy(b, source):
+        relayed = b in RELAYED
+        return pltpu.make_async_remote_copy(
+            src_ref=source.at[part(b)],
+            dst_ref=relay_part(b) if relayed else stage.at[2, part(b)],
+            send_sem=part_send,
+            recv_sem=relay_recv.at[RELAYED.index(b)] if relayed else part_recv.at[third(b)],
+            device_id=(relay_by if relayed else neighbour, cell),
+            device_id_type=MESH,
+        )
+
+    def ship(*parts):
+        for turn, other in enumerate((up_hbm, down_hbm)):
+
+            @pl.when(jnp.logical_and(inner, way == turn))
+            def _():
+                for b in parts:
+                    ship_copy(b, other).start()
+
+    def hand_on(*parts):
+        @pl.when(rank < 2)
+        def _():
+            for b in parts:
+                all_of(relay_part(b), relay_recv.at[RELAYED.index(b)])
+                pltpu.make_async_remote_copy(
+                    src_ref=relay_part(b),
+                    dst_ref=stage.at[2, part(b)],
+                    send_sem=part_send,
+                    recv_sem=part_recv.at[third(b)],
+                    device_id=(across, cell),
+                    device_id_type=MESH,
+                ).start()
+
     def own_sweep(turn, meanwhile):
-        for j in range(group):
-            pltpu.make_async_copy(fwd_rcv.at[turn, j], fwd_rcv.at[turn, j], fwd_recv.at[turn, j]).wait()
+        all_of(fwd_rcv.at[turn], fwd_recv.at[turn])
         right = jnp.zeros((8, width), F32)
         left = jnp.zeros((8, width), F32)
         for j in range(group):
@@ -269,106 +344,171 @@
         return pl.ds(index * chunk, chunk)
 
     def collected(turn, index):
-        for part in range(owners):
-            owner = index + CHUNKS * part
-            ref = bwd_rcv.at[turn, *piece(owner)]
-            pltpu.make_async_copy(ref, ref, bwd_recv.at[turn, owner]).wait()
         rows = chunk_rows(index)
+        all_of(bwd_rcv.at[turn, rows], bwd_recv.at[turn, index])
         return anchor[rows, :] + lateral_weight * bwd_rcv[turn, rows, :]
 
-    def prepare_down():
-        loads[5].wait()
-        for b in range(3):
-            prepare(1, b, dep_high.at[0], dep_low.at[0])
-
-    def prepare_up():
-        loads[6].wait()
-        for b in range(3):
-            prepare(2, b, dep_high.at[1], dep_low.at[1])
-
-    prepare_down()
+    def prepare_main():
+        @pl.when(rank > 0)
+        def _():
+            operator_load(down_hbm, 1).wait()
+            for b in range(3):
+                prepare(1, b, dep_high.at[0], dep_low.at[0])
+
+    def prepare_other(b):
+        all_of(stage.at[2, pl.ds(b * block, block)], part_recv.at[b])
+        prepare(2, b, dep_high.at[1], dep_low.at[1])
+
+    def first_meanwhile():
+        ship(2, 3, 4)
+
+        @pl.when(rank == 1)
+        def _():
+            operator_load(down_hbm, 2).wait()
+            for b in range(3):
+                prepare(2, b, dep_high.at[1], dep_low.at[1])
+
+    def second_meanwhile():
+        ship(7, 8, 9)
+        hand_on(6)
+
+        @pl.when(inner)
+        def _():
+            prepare_other(0)
+
+    ship(1, 0)
+    prepare_main()
     damping()
-    own_sweep(0, prepare_up)
+    own_sweep(0, first_meanwhile)
+    ship(5, 6)
+    hand_on(1)
     for index in range(CHUNKS):
         rows = chunk_rows(index)
         fwd_src[1, rows, :] = product(collected(0, index), lat_high[...], lat_low[...])
         send_forward(1, index)
-    own_sweep(1, lambda: None)
-
-    first = jnp.where(layer >= layers // 2, 1, 0)
-    second = 1 - first
-    place = jnp.where(first == 0, layer, layers - 1 - layer)
+    hand_on(5)
+    own_sweep(1, second_meanwhile)
+    ship(10, 11)
+
+    @pl.when(inner)
+    def _():
+        prepare_other(1)
 
     def depth_chunk(k):
         return pl.ds(pl.multiple_of(k * depth_rows, 8), depth_rows)
 
-    def depth_copy(source, way, k):
+    def depth_copy(source, k, send, slot, target):
         rows = depth_chunk(k)
         return pltpu.make_async_remote_copy(
             src_ref=source.at[rows],
-            dst_ref=dep_rcv.at[way, rows],
-            send_sem=dep_send.at[way, k],
-            recv_sem=dep_recv.at[way, k],
-            device_id=(layer + 1 - 2 * way, cell),
-            device_id_type=MESH,
-        )
-
-    def arrived(way, k):
-        ref = dep_rcv.at[way, depth_chunk(k)]
-        pltpu.make_async_copy(ref, ref, dep_recv.at[way, k]).wait()
-
-    def step(way, k):
-        rows = depth_chunk(k)
-        arrived(way, k)
-        dep_src[way, rows, :] = smooth[rows, :] + product(
-            dep_rcv[way, rows, :], dep_high[way], dep_low[way]
-        )
-        depth_copy(dep_src.at[way], way, k).start()
+            dst_ref=dep_rcv.at[slot, rows],
+            send_sem=dep_send.at[send],
+            recv_sem=dep_recv.at[slot, k],
+            device_id=(target, cell),
+            device_id_type=MESH,
+        )
+
+    def arrived(slot, k):
+        ref = dep_rcv.at[slot, depth_chunk(k)]
+        pltpu.make_async_copy(ref, ref, dep_recv.at[slot, k]).wait()
+
+    def mate_copy(index):
+        rows = chunk_rows(index)
+        return pltpu.make_async_remote_copy(
+            src_ref=smooth.at[rows],
+            dst_ref=mate.at[rows],
+            send_sem=mate_send,
+            recv_sem=mate_recv,
+            device_id=(neighbour, cell),
+            device_id_type=MESH,
+        )
 
     for index in range(CHUNKS):
         rows = chunk_rows(index)
         smooth[rows, :] = collected(1, index)
 
-        @pl.when(place == 0)
+        @pl.when(rank == 0)
         def _():
             for k in range(index * per_chunk, (index + 1) * per_chunk):
-                depth_copy(smooth, first, k).start()
-            out_ref[rows, :] = smooth[rows, :]
-
-        @pl.when(place > 0)
-        def _():
-            @pl.loop(index * per_chunk, (index + 1) * per_chunk)
-            def _(k):
-                step(first, k)
-
-            out_ref[rows, :] = smooth[rows, :] + depth_weight * dep_rcv[first, rows, :]
-
-    @pl.loop(0, DEPTH_CHUNKS)
-    def _(k):
-        @pl.when(place == 0)
-        def _():
-            arrived(second, k)
-
-        @pl.when(place > 0)
-        def _():
-            step(second, k)
-
-        rows = depth_chunk(k)
-        out_ref[rows, :] = out_ref[rows, :] + depth_weight * dep_rcv[second, rows, :]
-
-    for offset in range(1, group):
-        for turn in range(PASSES):
-            forward_copy(turn, peer(offset)).wait_send()
-            backward_copy(turn, peer(offset)).wait_send()
-        decay_copy(peer(offset)).wait_send()
+                depth_copy(smooth, k, 0, 0, chain_to).start()
+
+        @pl.when(inner)
+        def _():
+            mate_copy(index).start()
+
+    hand_on(10, 11)
+
+    def applied(c, which):
+        return product(c, dep_high[which], dep_low[which])
+
+    @pl.when(rank == 1)
+    def _():
+        @pl.loop(0, DEPTH_CHUNKS)
+        def _(k):
+            rows = depth_chunk(k)
+            arrived(0, k)
+            dep_src[0, rows, :] = smooth[rows, :] + applied(dep_rcv[0, rows, :], 0)
+            depth_copy(dep_src.at[0], k, 0, 0, chain_to).start()
+            out_ref[rows, :] = smooth[rows, :] + depth_weight * dep_rcv[0, rows, :]
+
+        @pl.loop(0, DEPTH_CHUNKS)
+        def _(k):
+            rows = depth_chunk(k)
+            arrived(1, k)
+            dep_src[1, rows, :] = smooth[rows, :] + applied(dep_rcv[1, rows, :], 1)
+            depth_copy(dep_src.at[1], k, 1, 1, back_to).start()
+            out_ref[rows, :] = out_ref[rows, :] + depth_weight * dep_rcv[1, rows, :]
+
+    @pl.when(rank == 0)
+    def _():
+        @pl.loop(0, DEPTH_CHUNKS)
+        def _(k):
+            rows = depth_chunk(k)
+            arrived(1, k)
+            out_ref[rows, :] = smooth[rows, :] + depth_weight * dep_rcv[1, rows, :]
+
+    @pl.when(inner)
+    def _():
+        prepare_other(2)
+        all_of(mate, mate_recv)
+
+        @pl.loop(0, DEPTH_CHUNKS)
+        def _(k):
+            rows = depth_chunk(k)
+            arrived(0, k)
+            near = smooth[rows, :] + applied(dep_rcv[0, rows, :], 0)
+            dep_src[0, rows, :] = near
+            dep_src[1, rows, :] = mate[rows, :] + applied(near, 1)
+            depth_copy(dep_src.at[1], k, 0, chain_slot, chain_to).start()
+            depth_copy(dep_src.at[0], k, 1, 1, neighbour).start()
+            out_ref[rows, :] = smooth[rows, :] + depth_weight * dep_rcv[0, rows, :]
+
+        @pl.loop(0, DEPTH_CHUNKS)
+        def _(k):
+            rows = depth_chunk(k)
+            arrived(1, k)
+            out_ref[rows, :] = out_ref[rows, :] + depth_weight * dep_rcv[1, rows, :]
+
+    peers = pl.ds(0, group - 1)
     for turn in range(PASSES):
-        carry_copy(turn).wait_send()
-    for k in range(DEPTH_CHUNKS):
-        depth_copy(smooth, first, k).wait_send()
-
-        @pl.when(place > 0)
-        def _():
-            depth_copy(smooth, second, k).wait_send()
+        all_of(fwd_rcv.at[turn, peers], fwd_send.at[turn])
+        all_of(bwd_src.at[turn, peers], bwd_send.at[turn])
+        all_of(car_src.at[turn], car_send.at[turn])
+    all_of(dec_rcv.at[peers], dec_send)
+    all_of(smooth, dep_send.at[0])
+
+    @pl.when(rank > 0)
+    def _():
+        all_of(smooth, dep_send.at[1])
+
+    @pl.when(inner)
+    def _():
+        all_of(smooth, mate_send)
+        all_of(stage.at[0], part_send)
+
+    @pl.when(rank < 2)
+    def _():
+        all_of(relay, part_send)
 
 
 def shards(source, rate, lat_op, down_op, up_op):
@@ -408,17 +548,24 @@
             vmem((columns, order), F32),
             vmem((2, columns, order), F32),
             vmem((2, columns, order), F32),
+            vmem((columns, order), F32),
+            vmem((len(RELAYED) * (order // PARTS), order), F32),
             dma((7,)),
-            dma((group,)),
-            dma((group,)),
-            dma((PASSES, group)),
-            dma((PASSES, group)),
+            dma,
+            dma,
             dma((PASSES,)),
             dma((PASSES,)),
-            dma((PASSES, group)),
-            dma((PASSES, group)),
+            dma((PASSES,)),
+            dma((PASSES,)),
+            dma((PASSES,)),
+            dma((PASSES, CHUNKS)),
+            dma((2,)),
             dma((2, DEPTH_CHUNKS)),
-            dma((2, DEPTH_CHUNKS)),
+            dma,
+            dma,
+            dma,
+            dma((3,)),
+            dma((len(RELAYED),)),
         ],
         compiler_params=pltpu.CompilerParams(
             collective_id=0, has_side_effects=True, vmem_limit_bytes=60 << 20

time: 75.4 us -> 72 us (0.955)
  Pallas kernels: 73.4 us -> 70.2 us
    pallas_call x1, Pallas kernels: 73.4 us -> 70.2 us  [shards(): pl.pallas_call(functools.partial(kernel, layers, cells), name='sweeps', o...]
where the time goes in v3:
time: 72 us; the launch traced here: 71.9 us
  Pallas kernels  70.2 us (98%)
  local copies, waits for them, and re-layouts  1.62 us (2%)
    pallas_call x1, Pallas kernels, shards(): pl.pallas_call(functools.partial(kernel, layers, cells), name='sweeps', o...  70.2 us
    unnamed x1, local copies, waits for them, and re-layouts  1.62 us

profile of v3, /device:TPU:16, one launch (start us, length us, event | category | flops | bytes accessed | tf_op | source)
XLA Modules:
  0.0 71.9 jit_solution(6866311237653735758)
XLA Ops:
  0.0 70.2 %sweeps.1 = f32[64,768]{1,0:T(8,128)} custom-call(f32[64,768]{1,0:T(8,128)} %bitcast.14, f32[1,768]{1,0:T(1,128)} %bitcast.15, f32[768,768]{1,0:T(8,128)} %bitcast.10, f32[768,768]{1,0:T(8,128)} %bitcast.11, f32[768,768]{1,0:T(8,128)} %bitcast.12), custom_call_target="tpu_custom_call" | custom-call | tf_op jit(solution)/shard_map/sweeps/pallas_call | solution.py:523
  70.3 1.6 %copy.7 = f32[1,1,768,64]{2,3,1,0:T(8,128)} copy(f32[1,1,768,64]{2,3,1,0:T(8,128)} %bitcast.13) | data formatting | bytes 393216

commit v4 on v3

--- a/solution.py
+++ b/solution.py
@@ -568,7 +568,7 @@
             dma((len(RELAYED),)),
         ],
         compiler_params=pltpu.CompilerParams(
-            collective_id=0, has_side_effects=True, vmem_limit_bytes=60 << 20
+            collective_id=0, has_side_effects=True, vmem_limit_bytes=56200000
         ),
     )(
         source.reshape(order, columns).T,

time: 72 us -> 71 us (0.986)
    pallas_call x1, Pallas kernels: 70.2 us -> 69.5 us  [shards(): pl.pallas_call(functools.partial(kernel, layers, cells), name='sweeps', o...]
    unnamed x1 -> x3, local copies, waits for them, and re-layouts: 1.62 us -> 1.36 us
where the time goes in v4:
time: 71 us; the launch traced here: 70.9 us
  Pallas kernels  69.5 us (98%)
  local copies, waits for them, and re-layouts  1.36 us (2%)
    pallas_call x1, Pallas kernels, shards(): pl.pallas_call(functools.partial(kernel, layers, cells), name='sweeps', o...  69.5 us

profile of v4, /device:TPU:16, one launch (start us, length us, event | category | flops | bytes accessed | tf_op | source)
XLA Modules:
  0.0 70.9 jit_solution(10748380443858678996)
XLA Ops:
  0.0 0.0 copy-start
  0.0 0.7 copy-done
  0.7 69.5 %sweeps.1 = f32[64,768]{1,0:T(8,128)S(1)} custom-call(f32[64,768]{1,0:T(8,128)} %bitcast.15, f32[1,768]{1,0:T(1,128)S(1)} %bitcast.11, f32[768,768]{1,0:T(8,128)} %bitcast.12, f32[768,768]{1,0:T(8,128)} %bitcast.13, f32[768,768]{1,0:T(8,128)} %bitcast.14), custom_call_target="tpu_custom_call" | custom-call | tf_op jit(solution)/shard_map/sweeps/pallas_call | solution.py:523
  70.2 0.7 copy.7
Async XLA Ops:
  0.0 0.7 copy-start

commit v5 on v4

--- a/solution.py
+++ b/solution.py
@@ -11,7 +11,7 @@
 CHUNKS = 2
 DEPTH_CHUNKS = 4
 PARTS = 12
-RELAYED = (1, 5, 6, 10, 11)
+RELAYED = (1, 5, 6, 10, 11,)
 
 lateral_weight = 0.1
 depth_weight = 0.25
@@ -360,7 +360,7 @@
         prepare(2, b, dep_high.at[1], dep_low.at[1])
 
     def first_meanwhile():
-        ship(2, 3, 4)
+        ship(2, 3, 4, 7)
 
         @pl.when(rank == 1)
         def _():
@@ -369,7 +369,7 @@
                 prepare(2, b, dep_high.at[1], dep_low.at[1])
 
     def second_meanwhile():
-        ship(7, 8, 9)
+        ship(8, 9)
         hand_on(6)
 
         @pl.when(inner)
@@ -386,9 +386,11 @@
         rows = chunk_rows(index)
         fwd_src[1, rows, :] = product(collected(0, index), lat_high[...], lat_low[...])
         send_forward(1, index)
+    ship(10)
     hand_on(5)
     own_sweep(1, second_meanwhile)
-    ship(10, 11)
+    ship(11)
+    hand_on(10)
 
     @pl.when(inner)
     def _():
@@ -418,7 +420,7 @@
             src_ref=smooth.at[rows],
             dst_ref=mate.at[rows],
             send_sem=mate_send,
-            recv_sem=mate_recv,
+            recv_sem=mate_recv.at[index],
             device_id=(neighbour, cell),
             device_id_type=MESH,
         )
@@ -436,7 +438,7 @@
         def _():
             mate_copy(index).start()
 
-    hand_on(10, 11)
+    hand_on(11)
 
     def applied(c, which):
         return product(c, dep_high[which], dep_low[which])
@@ -470,14 +472,18 @@
     @pl.when(inner)
     def _():
         prepare_other(2)
-        all_of(mate, mate_recv)
-
         @pl.loop(0, DEPTH_CHUNKS)
         def _(k):
             rows = depth_chunk(k)
             arrived(0, k)
             near = smooth[rows, :] + applied(dep_rcv[0, rows, :], 0)
             dep_src[0, rows, :] = near
+            for index in range(CHUNKS):
+
+                @pl.when(k == index * per_chunk)
+                def _():
+                    all_of(mate.at[chunk_rows(index)], mate_recv.at[index])
+
             dep_src[1, rows, :] = mate[rows, :] + applied(near, 1)
             depth_copy(dep_src.at[1], k, 0, chain_slot, chain_to).start()
             depth_copy(dep_src.at[0], k, 1, 1, neighbour).start()
@@ -562,7 +568,7 @@
             dma((2,)),
             dma((2, DEPTH_CHUNKS)),
             dma,
-            dma,
+            dma((CHUNKS,)),
             dma,
             dma((3,)),
             dma((len(RELAYED),)),

time: 71 us -> 68 us (0.958)
  Pallas kernels: 69.5 us -> 66.5 us
    pallas_call x1, Pallas kernels: 69.5 us -> 66.5 us  [shards(): pl.pallas_call(functools.partial(kernel, layers, cells), name='sweeps', o...]
where the time goes in v5:
time: 68 us; the launch traced here: 67.9 us
  Pallas kernels  66.5 us (98%)
  local copies, waits for them, and re-layouts  1.36 us (2%)
    pallas_call x1, Pallas kernels, shards(): pl.pallas_call(functools.partial(kernel, layers, cells), name='sweeps', o...  66.5 us
    unnamed x3, local copies, waits for them, and re-layouts  1.36 us

profile of v5, /device:TPU:16, one launch (start us, length us, event | category | flops | bytes accessed | tf_op | source)
XLA Modules:
  0.0 67.9 jit_solution(18319753009513696370)
XLA Ops:
  0.0 0.0 copy-start
  0.0 0.7 %copy-done = f32[1,1,768]{2,1,0:T(1,128)S(1)} copy-done((f32[1,1,768]{2,1,0:T(1,128)S(1)}, f32[1,1,768]{2,1,0:T(1,128)}, u32[]{:S(2)}) %copy-start) | copy-done | bytes 3096
  0.7 66.5 %sweeps.1 = f32[64,768]{1,0:T(8,128)S(1)} custom-call(f32[64,768]{1,0:T(8,128)} %bitcast.15, f32[1,768]{1,0:T(1,128)S(1)} %bitcast.11, f32[768,768]{1,0:T(8,128)} %bitcast.12, f32[768,768]{1,0:T(8,128)} %bitcast.13, f32[768,768]{1,0:T(8,128)} %bitcast.14), custom_call_target="tpu_custom_call" | custom-call | tf_op jit(solution)/shard_map/sweeps/pallas_call | solution.py:529
  67.2 0.7 %copy.7 = f32[1,1,768,64]{2,3,1,0:T(8,128)} copy(f32[1,1,768,64]{2,3,1,0:T(8,128)S(1)} %bitcast.10) | data formatting | bytes 393216
Async XLA Ops:
  0.0 0.7 %copy-start = (f32[1,1,768]{2,1,0:T(1,128)S(1)}, f32[1,1,768]{2,1,0:T(1,128)}, u32[]{:S(2)}) copy-start(f32[1,1,768]{2,1,0:T(1,128)} %param.6) | copy-start | bytes 9220
